TPU v7x, 256 devices: a whole 4x4x8 slice. The times are simulated.
256 devices in a mesh: freq: 8 (over x, z_hi), panel: 32 (over z_lo, y, core).
Axes of the slice: x: 4, y: 4, z: 8 (z_hi: 2, z_lo: 4; z = z_hi * 4 + z_lo), core: 2. Of those that a mesh axis runs over, the one named last changes fastest.
Arguments:
- load_history: bfloat16 [4096, 4096], P('freq', 'panel'), may hold values from -6 to 6
- source_blade: int32 [4096], P('panel'), may hold values from 0 to 3
- source_position: float32 [3, 4096], replicated, may hold values from -1 to 1
- airframe_position: float32 [3, 4096], replicated, may hold values from -1 to 1
- airframe_reflect: float32 [4096], P('panel'), may hold values from 0.5 to 2
- observer_position: float32 [3, 4096], replicated, may hold values from -1 to 1
- observer_near: int32 [4096, 4], replicated, may hold values from 0 to 4095
Outputs:
- observer_time: float32 [4096, 4096], P('freq', 'panel')
Inputs may be any that keep to these rules, and one draw needn't show every extreme that they name: `observer_near`: an airframe panel may appear more than once in a list.
All inputs are finite; a program needn't handle non-finite values.
Results may differ from a plain program's by a relative error of at most 0.0024.
Values sent between devices are 32-bit elements; how exact they have to be, the bound alone decides.
A program may use at most 64 MiB of HBM per device.

v0:
```python
import math

import jax
import jax.numpy as jnp
from jax import lax
from jax.sharding import PartitionSpec as P

TIMES = 4096
FREQS = 128
BLADES = 4
O_DEV = 128


wave_base = 8.0
wave_step = 0.15
near_gain = 0.5
hub_height = 3.0
ground_depth = -4.0


def split_up(x, dim, devices):
    before, after = (x.shape[:dim], x.shape[dim + 1 :])
    return jnp.moveaxis(x.reshape(*before, devices, -1, *after), dim, 0)


def sent_and_summed(x, axis, dim):
    parts = split_up(x, dim, lax.axis_size(axis))
    arrived = lax.all_to_all(parts, axis, split_axis=0, concat_axis=0, tiled=True)
    return arrived.sum(axis=0)


def laid_out(parts, dim):
    shape = list(parts.shape[1:])
    shape[dim] *= parts.shape[0]
    return jnp.moveaxis(parts, 0, dim).reshape(shape)


def from_everyone(x, axis):
    copies = jnp.broadcast_to(x, (lax.axis_size(axis), *x.shape))
    return lax.all_to_all(copies, axis, split_axis=0, concat_axis=0, tiled=True)


def gather_directly(x, axis, dim):
    return laid_out(from_everyone(x, axis), dim)


def lifted(position, height):
    return position + jnp.array([0.0, 0.0, height], jnp.float32)[:, None]


def distances(targets, anchors):
    offset_vec = targets[:, :, None] - anchors[:, None, :]
    return jnp.sqrt(jnp.sum(offset_vec * offset_vec, axis=0))


def radiate(wave_numbers, spread, source):
    inverse = 1.0 / (4.0 * math.pi * spread)
    phase_angle = wave_numbers[:, None, None] * spread[None]
    real_part = jnp.cos(phase_angle) * inverse
    imag_part = -jnp.sin(phase_angle) * inverse
    out_re = jnp.sum(real_part * source[0][:, None, :] - imag_part * source[1][:, None, :], axis=2)
    out_im = jnp.sum(real_part * source[1][:, None, :] + imag_part * source[0][:, None, :], axis=2)
    return jnp.stack([out_re, out_im])


def radiate_grouped(wave_numbers, spread, source, group_limit):
    freq_total = wave_numbers.shape[0]
    group_size = math.gcd(group_limit, freq_total)
    block_total = freq_total // group_size
    wave_blocks = wave_numbers.reshape(block_total, group_size)
    source_blocks = jnp.moveaxis(source.reshape(2, block_total, group_size, source.shape[2]), 1, 0)
    result = lax.map(
        lambda entry_pair: radiate(entry_pair[0], spread, entry_pair[1]),
        (wave_blocks, source_blocks),
    )
    return jnp.moveaxis(result, 0, 1).reshape(2, freq_total, spread.shape[0])


def on_device(
    load_history,
    source_blade,
    source_position,
    airframe_position,
    airframe_reflect,
    observer_position,
    observer_near,
):
    freq_index = lax.axis_index("freq")
    panel_index = lax.axis_index("panel")
    freq_share = FREQS // lax.axis_size("freq")
    time_rows = load_history.shape[0]
    air_rows = airframe_reflect.shape[0]
    obs_rows = O_DEV
    harmonic = jnp.arange(1, FREQS + 1, dtype=jnp.int32)
    time_steps = freq_index * time_rows + jnp.arange(time_rows, dtype=jnp.int32)
    forward_angle = (harmonic[:, None] * time_steps[None, :] % TIMES).astype(jnp.float32) * (
        2.0 * math.pi / TIMES
    )
    cos_table = jnp.cos(forward_angle).astype(jnp.bfloat16)
    sin_table = jnp.sin(forward_angle).astype(jnp.bfloat16)
    partial_re = jnp.dot(cos_table, load_history, preferred_element_type=jnp.float32)
    partial_im = -jnp.dot(sin_table, load_history, preferred_element_type=jnp.float32)
    partial_terms = jnp.stack([partial_re, partial_im])
    owned = sent_and_summed(partial_terms, "freq", 1)
    owned = owned * TIMES ** (-0.5)
    own_harmonic = freq_index * freq_share + 1 + jnp.arange(freq_share, dtype=jnp.int32)
    blade_angle = (own_harmonic[:, None] * source_blade[None, :] % BLADES).astype(jnp.float32) * (
        2.0 * math.pi / BLADES
    )
    rotated_re = owned[0] * jnp.cos(blade_angle) + owned[1] * jnp.sin(blade_angle)
    rotated_im = owned[1] * jnp.cos(blade_angle) - owned[0] * jnp.sin(blade_angle)
    rotated = jnp.stack([rotated_re, rotated_im])
    wave_numbers = wave_base + wave_step * (own_harmonic - 1).astype(jnp.float32)
    sources_all = lifted(source_position, hub_height)
    air_local = lax.dynamic_slice_in_dim(airframe_position, panel_index * air_rows, air_rows, 1)
    shard_block = gather_directly(rotated, "panel", 2)
    anchors = sources_all
    incident = radiate_grouped(wave_numbers, distances(air_local, anchors), shard_block, 8)
    scattered = incident * airframe_reflect[None, None, :]
    observers_all = lifted(observer_position, ground_depth)
    obs_local = lax.dynamic_slice_in_dim(observers_all, panel_index * obs_rows, obs_rows, 1)
    near_local = lax.dynamic_slice_in_dim(observer_near, panel_index * obs_rows, obs_rows, 0)
    shard_block = gather_directly(scattered, "panel", 2)
    piece_cols = shard_block.shape[2]
    anchors = airframe_position
    far_field = radiate_grouped(wave_numbers, distances(obs_local, anchors), shard_block, 8)
    columns = jnp.arange(piece_cols, dtype=jnp.int32)
    hits = jnp.sum((near_local[:, :, None] == columns[None, None, :]).astype(jnp.float32), axis=1)
    near_field = jnp.einsum("pfw,ow->pfo", shard_block, hits, precision=lax.Precision.HIGHEST)
    observed = far_field + near_gain * near_field
    shard_block = gather_directly(observed, "freq", 1)
    piece_rows = shard_block.shape[1]
    harmonics = jnp.int32(0) + 1 + jnp.arange(piece_rows, dtype=jnp.int32)
    back_angle = (harmonics[:, None] * time_steps[None, :] % TIMES).astype(jnp.float32) * (
        2.0 * math.pi / TIMES
    )
    cosine_part = jnp.dot(jnp.cos(back_angle).T, shard_block[0], precision=lax.Precision.HIGHEST)
    sine_part = jnp.dot(jnp.sin(back_angle).T, shard_block[1], precision=lax.Precision.HIGHEST)
    series = cosine_part - sine_part
    return series * (2 * FREQS) ** (-0.5)


def solution(mesh):
    return jax.shard_map(
        on_device,
        mesh=mesh,
        in_specs=(P("freq", "panel"), P("panel"), P(), P(), P("panel"), P(), P()),
        out_specs=P("freq", "panel"),
        check_vma=False,
    )
```

profile of v0, /device:TPU:8, one launch (start us, length us, event | category | flops | bytes accessed | tf_op | source)
XLA Modules:
  0.0 358.7 jit_solution(8070705952409664000)
XLA Ops:
  0.9 1.1 fusion.41
  2.1 1.2 convolution_negate_fusion
  3.9 10.9 %all-to-all-start = ((f32[8,2,16,128]{3,2,1,0:T(8,128)}), f32[8,2,16,128]{3,2,1,0:T(8,128)S(1)}, u32[]{:S(2)}, u32[]{:S(2)}) async-start(f32[8,2,16,128]{3,2,1,0:T(8,128)} %maximum_bitcast_fusion.2), calls=%async_computation | async-start | bytes 262144 | tf_op jit(solution)/shard_map/all_to_all | solution.py:28
  15.6 9.8 %all-to-all-done = f32[8,2,16,128]{3,2,1,0:T(8,128)S(1)} async-done(((f32[8,2,16,128]{3,2,1,0:T(8,128)}), f32[8,2,16,128]{3,2,1,0:T(8,128)S(1)}, u32[]{:S(2)}, u32[]{:S(2)}) %all-to-all-start) | async-done | bytes 131104 | tf_op jit(solution)/shard_map/all_to_all | solution.py:28
  26.5 6.4 %all-to-all-start.1 = ((f32[32,2,16,128]{3,2,1,0:T(8,128)}), f32[32,2,16,128]{3,2,1,0:T(8,128)S(1)}, u32[]{:S(2)}, u32[]{:S(2)}) async-start(f32[32,2,16,128]{3,2,1,0:T(8,128)} %broadcast_in_dim.12), calls=%async_computation.1 | async-start | bytes 1048576 | tf_op jit(solution)/shard_map/all_to_all | solution.py:40
  33.0 0.9 multiply_reduce_fusion
  34.4 13.2 %all-to-all-done.1 = f32[32,2,16,128]{3,2,1,0:T(8,128)S(1)} async-done(((f32[32,2,16,128]{3,2,1,0:T(8,128)}), f32[32,2,16,128]{3,2,1,0:T(8,128)S(1)}, u32[]{:S(2)}, u32[]{:S(2)}) %all-to-all-start.1) | async-done | bytes 524320 | tf_op jit(solution)/shard_map/all_to_all | solution.py:40
  48.0 132.9 %while.20 = (s32[]{:T(128)}, f32[2,2,8,128]{3,2,0,1:T(8,128)S(1)}, f32[2,8]{1,0:T(2,128)S(1)}, f32[128,4096]{1,0:T(8,128)S(1)}, f32[2,2,8,4096]{3,2,0,1:T(8,128)S(1)}, /*index=5*/s32[]{:T(128)}) while((s32[]{:T(128)}, f32[2,2,8,128]{3,2,0,1:T(8,128)S(1)}, f32[2,8]{1,0:T(2,128)S(1)}, f32[128,4096]{1,0:T(8,128)S(1)}, ...), condition=%wide.region_5.6_spmd, body=%wide.region_2.5_spmd.sunk | while | flops 51380224 | bytes 9724081 | solution.py:72
  48.4 66.1 %fusion.85 = (f32[8,128]{1,0:T(8,128)S(1)}, f32[8,128]{1,0:T(8,128)S(1)}) fusion(f32[8,4096]{1,0:T(8,128)S(1)} %get-tuple-element.190, f32[8,4096]{1,0:T(8,128)S(1)} %get-tuple-element.191, f32[128,4096]{1,0:T(8,128)S(1)} %multiply_divide_fusion.4, f32[128,4096]{1,0:T(8,128)S(1)} %get-tuple-element.218, f32[8]{0:T(128)S(1)} %fusion.84), kind=kLoop, calls=%fused_computation.6.clone.1 | loop fusion | flops 50329600 | bytes 4464672 | tf_op jit(solution)/shard_map/while/body/eval_jaxpr/reduce_sum | solution.py:61
  114.8 66.1 %fusion.85 = (f32[8,128]{1,0:T(8,128)S(1)}, f32[8,128]{1,0:T(8,128)S(1)}) fusion(f32[8,4096]{1,0:T(8,128)S(1)} %get-tuple-element.190, f32[8,4096]{1,0:T(8,128)S(1)} %get-tuple-element.191, f32[128,4096]{1,0:T(8,128)S(1)} %multiply_divide_fusion.4, f32[128,4096]{1,0:T(8,128)S(1)} %get-tuple-element.218, f32[8]{0:T(128)S(1)} %fusion.84), kind=kLoop, calls=%fused_computation.6.clone.1 | loop fusion | flops 50329600 | bytes 4464672 | tf_op jit(solution)/shard_map/while/body/eval_jaxpr/reduce_sum | solution.py:61
  180.9 0.9 broadcast_in_dim.18
  181.8 5.9 %all-to-all-start.2 = ((f32[32,2,16,128]{3,2,1,0:T(8,128)}), f32[32,2,16,128]{3,2,1,0:T(8,128)S(1)}, u32[]{:S(2)}, u32[]{:S(2)}) async-start(f32[32,2,16,128]{3,2,1,0:T(8,128)} %broadcast_in_dim.18), calls=%async_computation.2 | async-start | bytes 1048576 | tf_op jit(solution)/shard_map/all_to_all | solution.py:40
  187.7 0.9 multiply_reduce_fusion.1
  189.7 2.8 convert_reduce_fusion
  192.5 9.8 %all-to-all-done.2 = f32[32,2,16,128]{3,2,1,0:T(8,128)S(1)} async-done(((f32[32,2,16,128]{3,2,1,0:T(8,128)}), f32[32,2,16,128]{3,2,1,0:T(8,128)S(1)}, u32[]{:S(2)}, u32[]{:S(2)}) %all-to-all-start.2) | async-done | bytes 524320 | tf_op jit(solution)/shard_map/all_to_all | solution.py:40
  202.3 1.1 copy.32
  203.4 1.1 reshape_reshape.7
  204.6 132.9 %while.21 = (s32[]{:T(128)}, f32[2,2,8,128]{3,2,1,0:T(8,128)S(1)}, f32[2,8]{1,0:T(2,128)S(1)}, f32[128,4096]{1,0:T(8,128)S(1)}, f32[2,2,8,4096]{3,2,0,1:T(8,128)S(1)}, /*index=5*/s32[]{:T(128)}) while((s32[]{:T(128)}, f32[2,2,8,128]{3,2,1,0:T(8,128)S(1)}, f32[2,8]{1,0:T(2,128)S(1)}, f32[128,4096]{1,0:T(8,128)S(1)}, ...), condition=%wide.region_10.11_spmd, body=%wide.region_7.10_spmd.sunk | while | flops 51380224 | bytes 9724081 | solution.py:72
  204.9 66.1 %fusion.88 = (f32[8,128]{1,0:T(8,128)S(1)}, f32[8,128]{1,0:T(8,128)S(1)}) fusion(f32[8,4096]{1,0:T(8,128)S(1)} %get-tuple-element.199, f32[8,4096]{1,0:T(8,128)S(1)} %get-tuple-element.200, f32[128,4096]{1,0:T(8,128)S(1)} %multiply_divide_fusion.5, f32[128,4096]{1,0:T(8,128)S(1)} %get-tuple-element.236, f32[8]{0:T(128)S(1)} %fusion.87), kind=kLoop, calls=%fused_computation.27.clone.1 | loop fusion | flops 50329600 | bytes 4464672 | tf_op jit(solution)/shard_map/while/body/eval_jaxpr/reduce_sum | solution.py:61
  271.4 66.1 %fusion.88 = (f32[8,128]{1,0:T(8,128)S(1)}, f32[8,128]{1,0:T(8,128)S(1)}) fusion(f32[8,4096]{1,0:T(8,128)S(1)} %get-tuple-element.199, f32[8,4096]{1,0:T(8,128)S(1)} %get-tuple-element.200, f32[128,4096]{1,0:T(8,128)S(1)} %multiply_divide_fusion.5, f32[128,4096]{1,0:T(8,128)S(1)} %get-tuple-element.236, f32[8]{0:T(128)S(1)} %fusion.87), kind=kLoop, calls=%fused_computation.27.clone.1 | loop fusion | flops 50329600 | bytes 4464672 | tf_op jit(solution)/shard_map/while/body/eval_jaxpr/reduce_sum | solution.py:61
  337.5 3.7 %fusion.32 = f32[2,16,128]{2,1,0:T(8,128)S(1)} fusion(f32[128,4096]{1,0:T(8,128)} %convert_reduce_fusion, f32[32,2,16,128]{3,2,1,0:T(8,128)S(1)} %all-to-all-done.2, f32[2,2,8,128]{3,2,1,0:T(8,128)S(1)} %get-tuple-element.60), kind=kOutput, calls=%fused_computation.52 | convolution fusion | flops 201334784 | bytes 2654208 | tf_op jit(solution)/shard_map/pfw,ow->pfo/dot_general | solution.py:129
  341.2 13.6 %all_to_all.20 = f32[8,2,16,128]{3,2,1,0:T(8,128)S(1)} all-to-all(f32[8,2,16,128]{3,2,1,0:T(8,128)S(1)} %broadcast_in_dim.19), channel_id=1, replica_groups=mesh['freq'=8,'panel'=32] {'freq'}, dimensions={0} | all-to-all | bytes 262144 | tf_op jit(solution)/shard_map/all_to_all | solution.py:40
  354.8 1.6 fusion.45
  356.4 2.3 fusion.28
  (56 shorter events, 6.9 us)
Async XLA Ops:
  0.0 0.9 copy-start
  0.0 14.8 %copy-start.6 = (f32[3]{0:T(128)S(1)}, f32[3]{0:T(128)}, u32[]{:S(2)}) copy-start(f32[3]{0:T(128)} %constant.109.clone) | copy-start | bytes 40
  0.0 14.8 %copy-start.1 = (f32[3,4096]{1,0:T(4,128)S(1)}, f32[3,4096]{1,0:T(4,128)}, u32[]{:S(2)}) copy-start(f32[3,4096]{1,0:T(4,128)} %param.16) | copy-start | bytes 147460
  0.0 25.4 %copy-start.3 = (s32[128]{0:T(128)S(1)}, s32[128]{0:T(128)}, u32[]{:S(2)}) copy-start(s32[128]{0:T(128)} %param.14) | copy-start | bytes 1540
  2.0 30.9 %copy-start.2 = (f32[3,4096]{1,0:T(4,128)S(1)}, f32[3,4096]{1,0:T(4,128)}, u32[]{:S(2)}) copy-start(f32[3,4096]{1,0:T(4,128)} %param.15) | copy-start | bytes 147460
  2.0 30.9 %copy-start.5 = (f32[3]{0:T(128)S(1)}, f32[3]{0:T(128)}, u32[]{:S(2)}) copy-start(f32[3]{0:T(128)} %constant.108.clone) | copy-start | bytes 40
  3.9 21.5 %all-to-all-start = ((f32[8,2,16,128]{3,2,1,0:T(8,128)}), f32[8,2,16,128]{3,2,1,0:T(8,128)S(1)}, u32[]{:S(2)}, u32[]{:S(2)}) async-start(f32[8,2,16,128]{3,2,1,0:T(8,128)} %maximum_bitcast_fusion.2), calls=%async_computation | async-start | bytes 262144 | tf_op jit(solution)/shard_map/all_to_all | solution.py:28
  26.5 21.1 %all-to-all-start.1 = ((f32[32,2,16,128]{3,2,1,0:T(8,128)}), f32[32,2,16,128]{3,2,1,0:T(8,128)S(1)}, u32[]{:S(2)}, u32[]{:S(2)}) async-start(f32[32,2,16,128]{3,2,1,0:T(8,128)} %broadcast_in_dim.12), calls=%async_computation.1 | async-start | bytes 1048576 | tf_op jit(solution)/shard_map/all_to_all | solution.py:40
  48.0 132.9 %copy-start.4 = (f32[128]{0:T(128)S(1)}, f32[128]{0:T(128)}, u32[]{:S(2)}) copy-start(f32[128]{0:T(128)} %param.17) | copy-start | bytes 1540
  181.8 20.5 %all-to-all-start.2 = ((f32[32,2,16,128]{3,2,1,0:T(8,128)}), f32[32,2,16,128]{3,2,1,0:T(8,128)S(1)}, u32[]{:S(2)}, u32[]{:S(2)}) async-start(f32[32,2,16,128]{3,2,1,0:T(8,128)} %broadcast_in_dim.18), calls=%async_computation.2 | async-start | bytes 1048576 | tf_op jit(solution)/shard_map/all_to_all | solution.py:40
where the time goes:
time: 361 us; the launch traced here: 359 us
  other arithmetic  272 us (75%)
  waiting for transfers between devices  32.8 us (9%)
  starting transfers between devices  23.2 us (6%)
  blocking collectives  13.6 us (4%)
  matrix products  9.85 us (3%)
  local copies, waits for them, and re-layouts  7.12 us (2%)
    reduce_sum x4, other arithmetic, radiate(): jnp.sum(real_part * source[0][:, None, :] - imag_part * source[1][:, None...  264 us
    all_to_all x2, waiting for transfers between devices, from_everyone(): return lax.all_to_all(copies, axis, split_axis=0, concat_axis=0, tiled=True)  23 us
    all_to_all x1, blocking collectives, from_everyone(): return lax.all_to_all(copies, axis, split_axis=0, concat_axis=0, tiled=True)  13.6 us
    all_to_all x2, starting transfers between devices, from_everyone(): return lax.all_to_all(copies, axis, split_axis=0, concat_axis=0, tiled=True)  12.3 us
    all_to_all x1, starting transfers between devices, sent_and_summed(): lax.all_to_all(parts, axis, split_axis=0, concat_axis=0, tiled=True)  10.9 us
    all_to_all x1, waiting for transfers between devices, sent_and_summed(): lax.all_to_all(parts, axis, split_axis=0, concat_axis=0, tiled=True)  9.81 us
  transfers between devices with their start and end apart: 3, of which 3 were waited for; matrix products, arithmetic and copies ran while one was open for 2% of the time, Pallas kernels for 0%

commit v1 on v0

v1 whole, which is shorter than its diff:
```python
import functools
import math

import jax
import jax.numpy as jnp
import numpy as np
from jax import lax
from jax.experimental import pallas as pl
from jax.experimental.pallas import tpu as pltpu
from jax.sharding import PartitionSpec as P

MESH = pl.DeviceIdType.MESH
F32, BF16 = jnp.float32, jnp.bfloat16
TIMES = 4096
PANELS = 32
LANES = 128
T_DEV = 512
F_DEV = 16
CHUNK = 4 * LANES
ROWS = 64


def fitted(fn, low, high, degree):
    cheb = np.polynomial.chebyshev.Chebyshev.interpolate(fn, degree, [low, high])
    return [float(v) for v in cheb.convert(kind=np.polynomial.Polynomial).coef]


COS_TURN = fitted(lambda u: np.cos(2 * np.pi * np.sqrt(u)), 1e-12, 0.25, 6)
SIN_TURN = fitted(lambda u: np.sin(2 * np.pi * np.sqrt(u)) / np.sqrt(u), 1e-12, 0.25, 5)
COS_HALF = fitted(lambda u: np.cos(0.075 * np.sqrt(u)), 0.99, 44.1, 3)
SIN_HALF = fitted(lambda u: np.sin(0.075 * np.sqrt(u)) / np.sqrt(u), 0.99, 44.1, 3)


def poly(coef, u):
    total = coef[-1] * u + coef[-2]
    for c in coef[-3::-1]:
        total = total * u + c
    return total


def row_freq(row):
    offset, base, side = (row // 8) % 4, (row // 4) % 2, (row // 2) % 2
    return 8 * base + jnp.where(side == 0, 4 + offset, 3 - offset)


def turn_cos(numbers):
    turn = (((numbers + 2048) & 4095) - 2048).astype(F32) * (1.0 / 4096.0)
    return poly(COS_TURN, turn * turn)


def swapped(v, even):
    n = v.shape[0]
    return jnp.where(even, pltpu.roll(v, n - 1, 0), pltpu.roll(v, 1, 0))


def body(
    load_ref, blade_ref, src_ref, air_ref, reflect_ref, obs_ref, near_ref, out_ref,
    table, part, recv_x, own, recv_z, gat1, gat2, spec, state1, state2, hits, back_hi, back_lo,
    column, weights,
    sx, rx, sz, rz, sy1, ry1, sc1, rc1, sl, rl, sy2, ry2, sc2, rc2, sf, rf,
):
    fi, pi = lax.axis_index("freq"), lax.axis_index("panel")
    x, zh = fi // 2, fi % 2
    zl, y, c = pi // 8, (pi // 2) % 4, pi % 2
    z = zh * 4 + zl

    def x_peer(d):
        return (((x + d) % 4) * 2 + zh, pi)

    def z_of(d):
        return (z + d) % 8

    def z_peer(d):
        zz = (z + d) % 8
        return (x * 2 + zz // 4, (zz % 4) * 8 + y * 2 + c)

    def y_peer(d):
        return (fi, zl * 8 + ((y + d) % 4) * 2 + c)

    def line_peer(d):
        return (fi, ((zl + d) % 4) * 8 + y * 2 + c)

    core_peer = (fi, zl * 8 + y * 2 + (1 - c))
    half_peer = (x * 2 + (1 - zh), pi)

    def send(src, dst, ssem, rsem, to):
        return pltpu.make_async_remote_copy(
            src_ref=src, dst_ref=dst, send_sem=ssem, recv_sem=rsem, device_id=to, device_id_type=MESH
        )

    barrier = pltpu.get_barrier_semaphore()
    peers = [x_peer(d) for d in (1, 2, 3)] + [z_peer(d) for d in range(1, 8)]
    peers += [y_peer(d) for d in (1, 2, 3)] + [core_peer]
    for to in peers:
        pl.semaphore_signal(barrier, inc=1, device_id=to, device_id_type=MESH)

    def table_rows(i, _):
        row = lax.broadcasted_iota(jnp.int32, (32, T_DEV), 0)
        t = lax.broadcasted_iota(jnp.int32, (32, T_DEV), 1) + fi * T_DEV
        m = i * F_DEV + row_freq(row) + 1
        table[pl.ds(pl.multiple_of(i * 32, 32), 32), :] = turn_cos(m * t + 1024 * (row % 2)).astype(BF16)
        return 0

    lax.fori_loop(0, 8, table_rows, 0)
    spectrum = jnp.dot(table[...], load_ref[...], preferred_element_type=F32) * (1.0 / 64.0)
    part[...] = spectrum.reshape(4, 64, LANES)

    pl.semaphore_wait(barrier, len(peers))

    x_sends = [
        send(part.at[(x + d) % 4], recv_x.at[d - 1], sx.at[d - 1], rx.at[d - 1], x_peer(d)) for d in (1, 2, 3)
    ]
    for s in x_sends:
        s.start()

    def setup(state, targets, anchors, lift, start, stop):
        wave = (8.0 + 0.15 * (F_DEV * fi.astype(F32) + 7.5)) * (1.0 / (2.0 * math.pi))
        at = pl.multiple_of(pi * LANES, LANES)
        tx, ty, tz = (targets[i : i + 1, pl.ds(at, LANES)] for i in range(3))

        def panel(k, _):
            dc, dy, zz = k // 16, (k // 4) % 4, k % 4
            p = zz * 8 + ((y - dy + 4) % 4) * 2 + (c + dc) % 2
            lane = pl.multiple_of(p * LANES, LANES)
            for i in range(3):
                row = jnp.broadcast_to(anchors[i : i + 1, pl.ds(lane, LANES)], (LANES, LANES))
                column[i] = row.T
            for h in range(LANES // ROWS):
                rows = pl.ds(h * ROWS, ROWS)
                dx, ddy, dz = tx - column[0, rows, :], ty - column[1, rows, :], (tz - lift) - column[2, rows, :]
                square = dx * dx + ddy * ddy + dz * dz
                inverse = lax.rsqrt(square)
                r = square * inverse
                turns = r * wave
                turns = turns - jnp.round(turns)
                u = turns * turns
                gain = inverse * (1.0 / (4.0 * math.pi))
                cp = poly(COS_TURN, u) * gain
                sp = poly(SIN_TURN, u) * turns * gain
                c0 = poly(COS_HALF, square)
                s0 = poly(SIN_HALF, square) * r
                twice = 4.0 * (c0 * c0) - 2.0
                c1, s1 = (twice - 1.0) * c0, (twice + 1.0) * s0
                c2, s2 = twice * c1 - c0, twice * s1 - s0
                c3, s3 = twice * c2 - c1, twice * s2 - s1
                cb, sb = c3 * c0 - s3 * s0, s3 * c0 + c3 * s0
                cc, ss, sc, cs = cp * cb, sp * sb, sp * cb, cp * sb
                dst = pl.ds(pl.multiple_of(k * LANES + h * ROWS, ROWS), ROWS)
                values = (cc + ss, sc - cs, cc - ss, sc + cs, c0, c1, c2, c3, s0, s1, s2, s3)
                for n, v in enumerate(values):
                    state[n, dst, :] = v.astype(BF16)
            return 0

        lax.fori_loop(start, stop, panel, 0)

    setup1 = functools.partial(setup, state1, air_ref, src_ref, 3.0)
    setup2 = functools.partial(setup, state2, obs_ref, air_ref, 4.0)

    setup1(0, 12)

    for s in x_sends:
        s.wait_recv()
    row = lax.broadcasted_iota(jnp.int32, (64, LANES), 0)
    even = row % 2 == 0
    total = part[x] + recv_x[0] + recv_x[1] + recv_x[2]
    quarter = ((row_freq(row) + 1) * blade_ref[...]) & 3
    cos_q = (quarter == 0).astype(F32) - (quarter == 2).astype(F32)
    sin_q = (quarter == 1).astype(F32) - (quarter == 3).astype(F32)
    turned = total * cos_q + swapped(total, even) * jnp.where(even, sin_q, -sin_q)
    own[...] = turned.reshape(2, 32, LANES)
    z_sends = [
        send(own.at[z_of(d) // 4], recv_z.at[z], sz.at[d - 1], rz.at[d - 1], z_peer(d)) for d in range(1, 8)
    ]
    for s in z_sends:
        s.start()
    recv_z[z] = own[zh]

    setup1(12, 32)

    for s in z_sends:
        s.wait_recv()
    gat1[c, y] = recv_z[0:4] + recv_z[4:8]

    def spread(gat, sy, ry, sc, rc):
        y_sends = [send(gat.at[c, y], gat.at[c, y], sy.at[d - 1], ry.at[d - 1], y_peer(d)) for d in (1, 2, 3)]
        for s in y_sends:
            s.start()
        c_sends = [
            send(gat.at[c, (y - d + 4) % 4], gat.at[c, (y - d + 4) % 4], sc.at[d], rc.at[d], core_peer)
            for d in range(4)
        ]
        c_sends[0].start()
        return y_sends, c_sends

    def forward(y_sends, c_sends):
        for d in (1, 2, 3):
            y_sends[d - 1].wait_recv()
            c_sends[d].start()

    y_sends, c_sends = spread(gat1, sy1, ry1, sc1, rc1)
    setup2(0, 12)
    forward(y_sends, c_sends)

    def radiate(gat, state, c_sends, near):
        row = lax.broadcasted_iota(jnp.int32, (32, LANES), 0)
        even = row % 2 == 0
        side = jnp.where((row // 2) % 2 == 0, 1.0, -1.0).astype(F32)
        acc = tuple(jnp.zeros((16, 256), F32) for _ in range(4))
        near_acc = jnp.zeros((64, LANES), F32)
        for dc in range(2):
            for dy in range(4):
                if dc:
                    c_sends[dy].wait_recv()
                cc, yy = (c + dc) % 2, (y - dy + 4) % 4
                for zz in range(4):
                    v = gat[cc, yy, zz]
                    hi = v.astype(BF16).astype(F32)
                    lo = v - hi
                    kinds = []
                    for part_ in (hi, lo):
                        sw = swapped(part_, even)
                        sw = jnp.where(even, sw, -sw)
                        kinds.append((part_, part_ * -side, sw, sw * side))
                    for kind in range(4):
                        for jj in range(4):
                            pair = jnp.concatenate([q[kind][8 * jj : 8 * jj + 8] for q in kinds], axis=0)
                            weights[
                                zz // 2, jj, :, kind * 256 + (zz % 2) * LANES : kind * 256 + (zz % 2 + 1) * LANES
                            ] = pair.astype(BF16)

                def tile(kt, carry):
                    acc, near_acc = carry
                    rows = pl.ds(pl.multiple_of((dc * 4 + dy) * CHUNK + kt * 256, 256), 256)
                    ec0, es0, ec1, es1 = (state[n, rows, :] for n in range(4))
                    new = []
                    for jj in range(4):
                        cj, sj = state[4 + jj, rows, :], state[8 + jj, rows, :]
                        big = jnp.concatenate(
                            [
                                jnp.concatenate([ec0 * cj, ec1 * cj], axis=1),
                                jnp.concatenate([es0 * sj, es1 * sj], axis=1),
                                jnp.concatenate([es0 * cj, es1 * cj], axis=1),
                                jnp.concatenate([ec0 * sj, ec1 * sj], axis=1),
                            ],
                            axis=0,
                        )
                        new.append(acc[jj] + jnp.dot(weights[kt, jj], big, preferred_element_type=F32))
                    if near:
                        left = jnp.concatenate([weights[kt, jj, :, 0:256] for jj in range(4)], axis=0)
                        near_acc = near_acc + jnp.dot(left, hits[rows, :], preferred_element_type=F32)
                    return tuple(new), near_acc

                acc, near_acc = lax.fori_loop(0, 2, tile, (acc, near_acc))
        low = lax.broadcasted_iota(jnp.int32, (8, LANES), 0) < 4
        blocks = []
        for jj in range(4):
            both = acc[jj][0:8] + acc[jj][8:16]
            block = jnp.where(low, both[:, :LANES], both[:, LANES:])
            if near:
                block = block + near_acc[16 * jj : 16 * jj + 8] + near_acc[16 * jj + 8 : 16 * jj + 16]
            blocks.append(block)
        return jnp.concatenate(blocks, axis=0)

    incident = radiate(gat1, state1, c_sends, False)
    gat2[c, y, zl] = incident * reflect_ref[...]
    l_sends = [
        send(gat2.at[c, y, zl], gat2.at[c, y, zl], sl.at[d - 1], rl.at[d - 1], line_peer(d)) for d in (1, 2, 3)
    ]
    for s in l_sends:
        s.start()

    setup2(12, 32)

    for s in l_sends:
        s.wait_recv()
    y_sends2, c_sends2 = spread(gat2, sy2, ry2, sc2, rc2)

    lists = near_ref[:, pl.ds(pl.multiple_of(pi * LANES, LANES), LANES)]

    def count(k, _):
        dc, dy, zz = k // 16, (k // 4) % 4, k % 4
        p = zz * 8 + ((y - dy + 4) % 4) * 2 + (c + dc) % 2
        index = lax.broadcasted_iota(jnp.int32, (LANES, LANES), 0) + p * LANES
        total = jnp.zeros((LANES, LANES), F32)
        for n in range(4):
            total = total + jnp.where(index == lists[n : n + 1, :], 0.5, 0.0)
        hits[pl.ds(pl.multiple_of(k * LANES, LANES), LANES), :] = total.astype(BF16)
        return 0

    lax.fori_loop(0, PANELS, count, 0)

    def back_rows(i, _):
        col = lax.broadcasted_iota(jnp.int32, (32, 256), 1)
        t = lax.broadcasted_iota(jnp.int32, (32, 256), 0) + fi * T_DEV + i * 32
        m = (col // 32) * F_DEV + row_freq(col) + 1
        value = turn_cos(m * t + 1024 * (col % 2))
        hi = value.astype(BF16)
        dst = pl.ds(pl.multiple_of(i * 32, 32), 32)
        back_hi[dst, :] = hi
        back_lo[dst, :] = (value - hi.astype(F32)).astype(BF16)
        return 0

    lax.fori_loop(0, T_DEV // 32, back_rows, 0)

    forward(y_sends2, c_sends2)
    spec[fi] = radiate(gat2, state2, c_sends2, True)

    f_sends = [send(spec.at[fi], spec.at[fi], sf.at[0], rf.at[0], half_peer)]
    f_sends += [send(spec.at[fi], spec.at[fi], sf.at[d], rf.at[d], x_peer(d)) for d in (1, 2, 3)]
    other = x * 2 + (1 - zh)
    f_sends += [send(spec.at[other], spec.at[other], sf.at[3 + d], rf.at[3 + d], x_peer(d)) for d in (1, 2, 3)]
    for s in f_sends[:4]:
        s.start()
    f_sends[0].wait_recv()
    for s in f_sends[4:]:
        s.start()
    for s in f_sends[1:]:
        s.wait_recv()

    observed = spec[...].reshape(256, LANES) * (1.0 / 16.0)
    hi = observed.astype(BF16)
    lo = (observed - hi.astype(F32)).astype(BF16)
    wide = jnp.dot(back_hi[...], jnp.concatenate([hi, lo], axis=1), preferred_element_type=F32)
    narrow = jnp.dot(back_lo[...], hi, preferred_element_type=F32)
    out_ref[...] = wide[:, :LANES] + wide[:, LANES:] + narrow

    for s in x_sends + z_sends + y_sends + c_sends + l_sends + y_sends2 + c_sends2 + f_sends:
        s.wait_send()


def on_device(load, blade, source, airframe, reflect, observer, near):
    vmem = pl.BlockSpec(memory_space=pltpu.VMEM)
    dma = pltpu.SemaphoreType.DMA
    scratch = [
        pltpu.VMEM((256, T_DEV), BF16),
        pltpu.VMEM((4, 64, LANES), F32),
        pltpu.VMEM((3, 64, LANES), F32),
        pltpu.VMEM((2, 32, LANES), F32),
        pltpu.VMEM((8, 32, LANES), F32),
        pltpu.VMEM((2, 4, 4, 32, LANES), F32),
        pltpu.VMEM((2, 4, 4, 32, LANES), F32),
        pltpu.VMEM((8, 32, LANES), F32),
        pltpu.VMEM((12, 4096, LANES), BF16),
        pltpu.VMEM((12, 4096, LANES), BF16),
        pltpu.VMEM((4096, LANES), BF16),
        pltpu.VMEM((T_DEV, 256), BF16),
        pltpu.VMEM((T_DEV, 256), BF16),
        pltpu.VMEM((3, LANES, LANES), F32),
        pltpu.VMEM((2, 4, 16, 1024), BF16),
    ]
    scratch += [dma((n,)) for n in (3, 3, 7, 7, 3, 3, 4, 4, 3, 3, 3, 3, 4, 4, 7, 7)]
    return pl.pallas_call(
        body,
        out_shape=jax.ShapeDtypeStruct((T_DEV, LANES), F32),
        in_specs=[vmem] * 7,
        out_specs=vmem,
        scratch_shapes=scratch,
        compiler_params=pltpu.CompilerParams(
            collective_id=0, has_side_effects=True, vmem_limit_bytes=56 * 1024 * 1024
        ),
        name="rotor",
    )(load, blade.reshape(1, LANES), source, airframe, reflect.reshape(1, LANES), observer, near.T)


def solution(mesh):
    return jax.shard_map(
        on_device,
        mesh=mesh,
        in_specs=(P("freq", "panel"), P("panel"), P(), P(), P("panel"), P(), P()),
        out_specs=P("freq", "panel"),
        check_vma=False,
    )
```

time: 361 us -> 60.5 us (0.17)
  other arithmetic: 272 us -> 0 us
  Pallas kernels: 0 us -> 58.1 us
  waiting for transfers between devices: 32.8 us -> 0 us
  starting transfers between devices: 23.2 us -> 0 us
  blocking collectives: 13.6 us -> 0 us
  matrix products: 9.85 us -> 0 us
  local copies, waits for them, and re-layouts: 7.12 us -> 1.67 us
    reduce_sum x8 -> x0, other arithmetic: 269 us -> none  [the longest x4 264 us: radiate(): jnp.sum(real_part * source[0][:, None, :] - imag_part * source[1][:, None...]
    pallas_call x0 -> x1, Pallas kernels: none -> 58.1 us  [on_device(): pl.pallas_call(body, out_shape=jax.ShapeDtypeStruct((T_DEV, LANES), F32),...]
    all_to_all x3 -> x0, waiting for transfers between devices: 32.8 us -> none  [the longest x2 23 us: from_everyone(): return lax.all_to_all(copies, axis, split_axis=0, concat_axis=0, tiled=True)]
    all_to_all x3 -> x0, starting transfers between devices: 23.2 us -> none  [the longest x2 12.3 us: from_everyone(): return lax.all_to_all(copies, axis, split_axis=0, concat_axis=0, tiled=True)]
    all_to_all x1 -> x0, blocking collectives: 13.6 us -> none  [from_everyone(): return lax.all_to_all(copies, axis, split_axis=0, concat_axis=0, tiled=True)]
    dot_general x5 -> x0, matrix products: 9.85 us -> none  [the longest x1 3.71 us: on_device(): jnp.einsum('pfw,ow->pfo', shard_block, hits, precision=lax.Precision.HIGH...]
  transfers between devices with their start and end apart: 3 -> 0, of which waited for: 3 -> 0; matrix products, arithmetic and copies ran while one was open for 2% -> 0% of each run, Pallas kernels for 0% -> 0%
where the time goes in v1:
time: 60.5 us; the launch traced here: 59.8 us
  Pallas kernels  58.1 us (96%)
  local copies, waits for them, and re-layouts  1.67 us (3%)
    pallas_call x1, Pallas kernels, on_device(): pl.pallas_call(body, out_shape=jax.ShapeDtypeStruct((T_DEV, LANES), F32),...  58.1 us
    unnamed x1, local copies, waits for them, and re-layouts  1.67 us

profile of v1, /device:TPU:8, one launch (start us, length us, event | category | flops | bytes accessed | tf_op | source)
XLA Modules:
  0.0 59.8 jit_solution(2343509015645980038)
XLA Ops:
  0.0 58.1 %rotor.1 = f32[512,128]{1,0:T(8,128)} custom-call(bf16[512,128]{1,0:T(8,128)(2,1)} %load_ref.1, s32[1,128]{1,0:T(1,128)} %bitcast.4, f32[3,4096]{1,0:T(4,128)} %src_ref.1, f32[3,4096]{1,0:T(4,128)} %air_ref.1, f32[1,128]{1,0:T(1,128)} %bitcast.5, f32[3,4096]{1,0:T(4,128)} %obs_ref.1, s32[4,4096]{1,0:T(4,128)} %bitcast.3), custom_call_target="tpu_custom_call" | custom-call | tf_op jit(solution)/shard_map/rotor/pallas_call | solution.py:352
  58.2 1.7 %copy.9 = f32[512,128]{1,0:T(8,128)} copy(f32[512,128]{1,0:T(8,128)} %rotor.1) | data formatting | bytes 524288

commit v2 on v0

v2 whole, which is shorter than its diff:
```python
import functools
import math

import jax
import jax.numpy as jnp
import numpy as np
from jax import lax
from jax.experimental import pallas as pl
from jax.experimental.pallas import tpu as pltpu
from jax.sharding import PartitionSpec as P

MESH = pl.DeviceIdType.MESH
F32, BF16 = jnp.float32, jnp.bfloat16
TIMES = 4096
PANELS = 32
LANES = 128
T_DEV = 512
F_DEV = 16
CUT = (20, 8, 24)
ROWS = 64


def fitted(fn, low, high, degree):
    cheb = np.polynomial.chebyshev.Chebyshev.interpolate(fn, degree, [low, high])
    return [float(v) for v in cheb.convert(kind=np.polynomial.Polynomial).coef]


COS_TURN = fitted(lambda u: np.cos(2 * np.pi * np.sqrt(u)), 1e-12, 0.25, 6)
SIN_TURN = fitted(lambda u: np.sin(2 * np.pi * np.sqrt(u)) / np.sqrt(u), 1e-12, 0.25, 5)
COS_HALF = fitted(lambda u: np.cos(0.075 * np.sqrt(u)), 0.99, 44.1, 3)
SIN_HALF = fitted(lambda u: np.sin(0.075 * np.sqrt(u)) / np.sqrt(u), 0.99, 44.1, 3)


def poly(coef, u):
    total = coef[-1] * u + coef[-2]
    for c in coef[-3::-1]:
        total = total * u + c
    return total


def row_freq(row):
    offset, base, side = (row // 8) % 4, (row // 4) % 2, (row // 2) % 2
    return 8 * base + jnp.where(side == 0, 4 + offset, 3 - offset)


def turn_cos(numbers):
    turn = (((numbers + 2048) & 4095) - 2048).astype(F32) * (1.0 / 4096.0)
    return poly(COS_TURN, turn * turn)


def swapped(v, even):
    n = v.shape[0]
    return jnp.where(even, pltpu.roll(v, n - 1, 0), pltpu.roll(v, 1, 0))


def body(
    load_ref, blade_ref, src_ref, air_ref, reflect_ref, obs_ref, near_ref, out_ref,
    part, recv_x, own, recv_z, mine1, recv1, line2, mine2, recv2, spec,
    sx, rx, sz, rz, s1, r1, sl, rl, s2, r2, sf, rf,
):
    fi, pi = lax.axis_index("freq"), lax.axis_index("panel")
    x, zh = fi // 2, fi % 2
    zl, y, c = pi // 8, (pi // 2) % 4, pi % 2
    z = zh * 4 + zl

    def x_peer(d):
        return (((x + d) % 4) * 2 + zh, pi)

    def z_of(d):
        return (z + d) % 8

    def z_peer(d):
        zz = (z + d) % 8
        return (x * 2 + zz // 4, (zz % 4) * 8 + y * 2 + c)

    def line_peer(d):
        return (fi, ((zl + d) % 4) * 8 + y * 2 + c)

    def block_panel(i):
        q = i // 2
        dy = (2 + q + q // 2 + 2 * (q // 3)) % 4
        return zl * 8 + ((y + dy) % 4) * 2 + (c + 1 - i % 2) % 2

    half_peer = (x * 2 + (1 - zh), pi)

    def send(src, dst, ssem, rsem, to):
        return pltpu.make_async_remote_copy(
            src_ref=src, dst_ref=dst, send_sem=ssem, recv_sem=rsem, device_id=to, device_id_type=MESH
        )

    barrier = pltpu.get_barrier_semaphore()
    peers = [x_peer(d) for d in (1, 2, 3)] + [z_peer(d) for d in range(1, 8)]
    peers += [(fi, block_panel(i)) for i in range(7)]
    for to in peers:
        pl.semaphore_signal(barrier, inc=1, device_id=to, device_id_type=MESH)

    def work(table, state1, state2, hits, back_hi, back_lo, column1, column2, weights):
        def table_rows(i, _):
            row = lax.broadcasted_iota(jnp.int32, (32, T_DEV), 0)
            t = lax.broadcasted_iota(jnp.int32, (32, T_DEV), 1) + fi * T_DEV
            m = i * F_DEV + row_freq(row) + 1
            table[pl.ds(pl.multiple_of(i * 32, 32), 32), :] = turn_cos(m * t + 1024 * (row % 2)).astype(BF16)
            return 0

        lax.fori_loop(0, 8, table_rows, 0)
        spectrum = jnp.dot(table[...], load_ref[...], preferred_element_type=F32) * (1.0 / 64.0)
        part[...] = spectrum.reshape(4, 64, LANES)

        def columns(column, anchors):
            def one(zz, _):
                lane = pl.multiple_of((zz * 8 + y * 2 + c) * LANES, LANES)
                for i in range(3):
                    row = jnp.broadcast_to(anchors[i : i + 1, pl.ds(lane, LANES)], (LANES, LANES))
                    column[zz, i] = row.T
                return 0

            lax.fori_loop(0, 4, one, 0)

        wave = (8.0 + 0.15 * (F_DEV * fi.astype(F32) + 7.5)) * (1.0 / (2.0 * math.pi))

        def setup(state, targets, column, lift, start, stop):
            def panel(k, _):
                zz = k % 4
                at = pl.multiple_of(block_panel(k // 4) * LANES, LANES)
                tx, ty, tz = (targets[i : i + 1, pl.ds(at, LANES)] for i in range(3))
                tz = tz - lift
                for h in range(LANES // ROWS):
                    rows = pl.ds(h * ROWS, ROWS)
                    dx, dy, dz = tx - column[zz, 0, rows, :], ty - column[zz, 1, rows, :], tz - column[zz, 2, rows, :]
                    square = dx * dx + dy * dy + dz * dz
                    inverse = lax.rsqrt(square)
                    r = square * inverse
                    turns = r * wave
                    turns = turns - jnp.round(turns)
                    u = turns * turns
                    gain = inverse * (1.0 / (4.0 * math.pi))
                    cp = poly(COS_TURN, u) * gain
                    sp = poly(SIN_TURN, u) * (turns * gain)
                    c0 = poly(COS_HALF, square)
                    s0 = poly(SIN_HALF, square) * r
                    twice = 4.0 * (c0 * c0) - 2.0
                    c1, s1_ = (twice - 1.0) * c0, (twice + 1.0) * s0
                    c2, s2_ = twice * c1 - c0, twice * s1_ - s0
                    c3, s3 = twice * c2 - c1, twice * s2_ - s1_
                    cb, sb = c3 * c0 - s3 * s0, s3 * c0 + c3 * s0
                    cp, sp, cb, sb = (v.astype(BF16) for v in (cp, sp, cb, sb))
                    cc, ss, sc, cs = cp * cb, sp * sb, sp * cb, cp * sb
                    dst = pl.ds(pl.multiple_of(k * LANES + h * ROWS, ROWS), ROWS)
                    values = (cc + ss, sc - cs, cc - ss, sc + cs, c0, c1, c2, c3, s0, s1_, s2_, s3)
                    for n, v in enumerate(values):
                        state[n, dst, :] = v.astype(BF16)
                return 0

            lax.fori_loop(start, stop, panel, 0)

        setup1 = functools.partial(setup, state1, air_ref, column1, 3.0)
        setup2 = functools.partial(setup, state2, obs_ref, column2, 4.0)
        columns(column1, src_ref)
        columns(column2, air_ref)

        setup1(0, CUT[0])
        pl.semaphore_wait(barrier, len(peers))

        x_sends = [
            send(part.at[(x + d) % 4], recv_x.at[d - 1], sx.at[d - 1], rx.at[d - 1], x_peer(d)) for d in (2, 1, 3)
        ]
        for s in x_sends:
            s.start()

        setup1(CUT[0], 32)
        setup2(0, CUT[1])

        for s in x_sends:
            s.wait_recv()
        row = lax.broadcasted_iota(jnp.int32, (64, LANES), 0)
        even = row % 2 == 0
        total = part[x] + recv_x[0] + recv_x[1] + recv_x[2]
        quarter = ((row_freq(row) + 1) * blade_ref[...]) & 3
        cos_q = (quarter == 0).astype(F32) - (quarter == 2).astype(F32)
        sin_q = (quarter == 1).astype(F32) - (quarter == 3).astype(F32)
        turned = total * cos_q + swapped(total, even) * jnp.where(even, sin_q, -sin_q)
        own[...] = turned.reshape(2, 32, LANES)
        z_sends = [
            send(own.at[z_of(d) // 4], recv_z.at[z], sz.at[d - 1], rz.at[d - 1], z_peer(d))
            for d in (4, 3, 5, 2, 6, 1, 7)
        ]
        for s in z_sends:
            s.start()
        recv_z[z] = own[zh]

        setup2(CUT[1], CUT[2])

        def radiate(line, state, mine, recv, ssem, rsem, near):
            row = lax.broadcasted_iota(jnp.int32, (32, LANES), 0)
            even = row % 2 == 0
            side = jnp.where((row // 2) % 2 == 0, 1.0, -1.0).astype(F32)
            for zz in range(4):
                v = line(zz)
                hi = v.astype(BF16).astype(F32)
                kinds = []
                for piece in (hi, v - hi):
                    sw = swapped(piece, even)
                    sw = jnp.where(even, sw, -sw)
                    kinds.append((piece, piece * -side, sw, sw * side))
                for kind in range(4):
                    for jj in range(4):
                        pair = jnp.concatenate([q[kind][8 * jj : 8 * jj + 8] for q in kinds], axis=0)
                        lane = kind * 256 + (zz % 2) * LANES
                        weights[zz // 2, jj, :, lane : lane + LANES] = pair.astype(BF16)
            low = lax.broadcasted_iota(jnp.int32, (8, LANES), 0) < 4

            def copy(i):
                return send(mine.at[i], recv.at[i], ssem.at[i], rsem.at[i], (fi, block_panel(i)))

            def block(i, _):
                acc = [jnp.zeros((16, 256), F32)] * 4
                near_acc = jnp.zeros((64, LANES), F32)
                for kt in range(2):
                    rows = pl.ds(pl.multiple_of(i * 512 + kt * 256, 256), 256)
                    ec0, es0, ec1, es1 = (state[n, rows, :] for n in range(4))
                    for jj in range(4):
                        cj, sj = state[4 + jj, rows, :], state[8 + jj, rows, :]
                        big = jnp.concatenate(
                            [
                                jnp.concatenate([ec0 * cj, ec1 * cj], axis=1),
                                jnp.concatenate([es0 * sj, es1 * sj], axis=1),
                                jnp.concatenate([es0 * cj, es1 * cj], axis=1),
                                jnp.concatenate([ec0 * sj, ec1 * sj], axis=1),
                            ],
                            axis=0,
                        )
                        acc[jj] = acc[jj] + jnp.dot(weights[kt, jj], big, preferred_element_type=F32)
                    if near:
                        left = jnp.concatenate([weights[kt, jj, :, 0:256] for jj in range(4)], axis=0)
                        near_acc = near_acc + jnp.dot(left, hits[rows, :], preferred_element_type=F32)
                for jj in range(4):
                    both = acc[jj][0:8] + acc[jj][8:16]
                    out = jnp.where(low, both[:, :LANES], both[:, LANES:])
                    if near:
                        out = out + near_acc[16 * jj : 16 * jj + 8] + near_acc[16 * jj + 8 : 16 * jj + 16]
                    mine[i, 8 * jj : 8 * jj + 8, :] = out

                @pl.when(i < 7)
                def _():
                    copy(i).start()

                return 0

            lax.fori_loop(0, 8, block, 0)
            copies = [copy(i) for i in range(7)]
            total = mine[7]
            for i in range(7):
                copies[i].wait_recv()
                total = total + recv[i]
            return total, copies

        for s in z_sends:
            s.wait_recv()
        incident, sends1 = radiate(lambda zz: recv_z[zz] + recv_z[zz + 4], state1, mine1, recv1, s1, r1, False)
        line2[zl] = incident * reflect_ref[...]
        l_sends = [
            send(line2.at[zl], line2.at[zl], sl.at[d - 1], rl.at[d - 1], line_peer(d)) for d in (2, 1, 3)
        ]
        for s in l_sends:
            s.start()

        setup2(CUT[2], 32)

        def count(k, _):
            at = pl.multiple_of(block_panel(k // 4) * LANES, LANES)
            first = ((k % 4) * 8 + y * 2 + c) * LANES
            index = lax.broadcasted_iota(jnp.int32, (LANES, LANES), 0)
            total = jnp.zeros((LANES, LANES), F32)
            for n in range(4):
                total = total + jnp.where(index == near_ref[n : n + 1, pl.ds(at, LANES)] - first, 0.5, 0.0)
            hits[pl.ds(pl.multiple_of(k * LANES, LANES), LANES), :] = total.astype(BF16)
            return 0

        lax.fori_loop(0, PANELS, count, 0)

        for s in l_sends:
            s.wait_recv()
        observed, sends2 = radiate(lambda zz: line2[zz], state2, mine2, recv2, s2, r2, True)
        spec[fi] = observed

        f_sends = [send(spec.at[fi], spec.at[fi], sf.at[0], rf.at[0], half_peer)]
        f_sends += [send(spec.at[fi], spec.at[fi], sf.at[d], rf.at[d], x_peer(d)) for d in (2, 1, 3)]
        other = x * 2 + (1 - zh)
        f_sends += [send(spec.at[other], spec.at[other], sf.at[3 + d], rf.at[3 + d], x_peer(d)) for d in (2, 1, 3)]
        for s in f_sends[:4]:
            s.start()

        def back_rows(i, _):
            col = lax.broadcasted_iota(jnp.int32, (32, 256), 1)
            t = lax.broadcasted_iota(jnp.int32, (32, 256), 0) + fi * T_DEV + i * 32
            m = (col // 32) * F_DEV + row_freq(col) + 1
            value = turn_cos(m * t + 1024 * (col % 2))
            hi = value.astype(BF16)
            dst = pl.ds(pl.multiple_of(i * 32, 32), 32)
            back_hi[dst, :] = hi
            back_lo[dst, :] = (value - hi.astype(F32)).astype(BF16)
            return 0

        lax.fori_loop(0, T_DEV // 32, back_rows, 0)
        f_sends[0].wait_recv()
        for s in f_sends[4:]:
            s.start()
        for s in f_sends[1:]:
            s.wait_recv()

        seen = spec[...].reshape(256, LANES) * (1.0 / 16.0)
        hi = seen.astype(BF16)
        lo = (seen - hi.astype(F32)).astype(BF16)
        wide = jnp.dot(back_hi[...], jnp.concatenate([hi, lo], axis=1), preferred_element_type=F32)
        narrow = jnp.dot(back_lo[...], hi, preferred_element_type=F32)
        out_ref[...] = wide[:, :LANES] + wide[:, LANES:] + narrow

        for s in x_sends + z_sends + sends1 + l_sends + sends2 + f_sends:
            s.wait_send()

    pl.run_scoped(
        work,
        pltpu.VMEM((256, T_DEV), BF16),
        pltpu.VMEM((12, 4096, LANES), BF16),
        pltpu.VMEM((12, 4096, LANES), BF16),
        pltpu.VMEM((4096, LANES), BF16),
        pltpu.VMEM((T_DEV, 256), BF16),
        pltpu.VMEM((T_DEV, 256), BF16),
        pltpu.VMEM((4, 3, LANES, LANES), F32),
        pltpu.VMEM((4, 3, LANES, LANES), F32),
        pltpu.VMEM((2, 4, 16, 1024), BF16),
    )


def on_device(load, blade, source, airframe, reflect, observer, near):
    vmem = pl.BlockSpec(memory_space=pltpu.VMEM)
    dma = pltpu.SemaphoreType.DMA
    slots = [(4, 64), (3, 64), (2, 32), (8, 32), (8, 32), (7, 32), (4, 32), (8, 32), (7, 32), (8, 32)]
    scratch = [pltpu.VMEM((*slot, LANES), F32) for slot in slots]
    scratch += [dma((n,)) for n in (3, 3, 7, 7, 7, 7, 3, 3, 7, 7, 7, 7)]
    return pl.pallas_call(
        body,
        out_shape=jax.ShapeDtypeStruct((T_DEV, LANES), F32),
        in_specs=[vmem] * 7,
        out_specs=vmem,
        scratch_shapes=scratch,
        compiler_params=pltpu.CompilerParams(
            collective_id=0, has_side_effects=True, vmem_limit_bytes=56 * 1024 * 1024
        ),
        name="rotor",
    )(load, blade.reshape(1, LANES), source, airframe, reflect.reshape(1, LANES), observer, near.T)


def solution(mesh):
    return jax.shard_map(
        on_device,
        mesh=mesh,
        in_specs=(P("freq", "panel"), P("panel"), P(), P(), P("panel"), P(), P()),
        out_specs=P("freq", "panel"),
        check_vma=False,
    )
```

time: 361 us -> 53.6 us (0.15)
  other arithmetic: 272 us -> 0 us
  Pallas kernels: 0 us -> 51.8 us
  waiting for transfers between devices: 32.8 us -> 0 us
  starting transfers between devices: 23.2 us -> 0 us
  blocking collectives: 13.6 us -> 0 us
  matrix products: 9.85 us -> 0 us
  local copies, waits for them, and re-layouts: 7.12 us -> 1.67 us
    reduce_sum x8 -> x0, other arithmetic: 269 us -> none  [the longest x4 264 us: radiate(): jnp.sum(real_part * source[0][:, None, :] - imag_part * source[1][:, None...]
    pallas_call x0 -> x1, Pallas kernels: none -> 51.8 us  [on_device(): pl.pallas_call(body, out_shape=jax.ShapeDtypeStruct((T_DEV, LANES), F32),...]
    all_to_all x3 -> x0, waiting for transfers between devices: 32.8 us -> none  [the longest x2 23 us: from_everyone(): return lax.all_to_all(copies, axis, split_axis=0, concat_axis=0, tiled=True)]
    all_to_all x3 -> x0, starting transfers between devices: 23.2 us -> none  [the longest x2 12.3 us: from_everyone(): return lax.all_to_all(copies, axis, split_axis=0, concat_axis=0, tiled=True)]
    all_to_all x1 -> x0, blocking collectives: 13.6 us -> none  [from_everyone(): return lax.all_to_all(copies, axis, split_axis=0, concat_axis=0, tiled=True)]
    dot_general x5 -> x0, matrix products: 9.85 us -> none  [the longest x1 3.71 us: on_device(): jnp.einsum('pfw,ow->pfo', shard_block, hits, precision=lax.Precision.HIGH...]
  transfers between devices with their start and end apart: 3 -> 0, of which waited for: 3 -> 0; matrix products, arithmetic and copies ran while one was open for 2% -> 0% of each run, Pallas kernels for 0% -> 0%
where the time goes in v2:
time: 53.6 us; the launch traced here: 53.5 us
  Pallas kernels  51.8 us (97%)
  local copies, waits for them, and re-layouts  1.67 us (3%)
    pallas_call x1, Pallas kernels, on_device(): pl.pallas_call(body, out_shape=jax.ShapeDtypeStruct((T_DEV, LANES), F32),...  51.8 us
    unnamed x1, local copies, waits for them, and re-layouts  1.67 us

profile of v2, /device:TPU:8, one launch (start us, length us, event | category | flops | bytes accessed | tf_op | source)
XLA Modules:
  0.0 53.5 jit_solution(4086649675102924985)
XLA Ops:
  0.0 51.8 %rotor.1 = f32[512,128]{1,0:T(8,128)} custom-call(bf16[512,128]{1,0:T(8,128)(2,1)} %load_ref.1, s32[1,128]{1,0:T(1,128)} %bitcast.4, f32[3,4096]{1,0:T(4,128)} %src_ref.1, f32[3,4096]{1,0:T(4,128)} %air_ref.1, f32[1,128]{1,0:T(1,128)} %bitcast.5, f32[3,4096]{1,0:T(4,128)} %obs_ref.1, s32[4,4096]{1,0:T(4,128)} %bitcast.3), custom_call_target="tpu_custom_call" | custom-call | tf_op jit(solution)/shard_map/rotor/pallas_call | solution.py:341
  51.8 1.7 %copy.9 = f32[512,128]{1,0:T(8,128)} copy(f32[512,128]{1,0:T(8,128)} %rotor.1) | data formatting | bytes 524288

commit v3 on v2

--- a/solution.py
+++ b/solution.py
@@ -16,7 +16,7 @@
 LANES = 128
 T_DEV = 512
 F_DEV = 16
-CUT = (20, 8, 24)
+CUT = (4, 1, 5)
 ROWS = 64
 
 
@@ -26,9 +26,11 @@
 
 
 COS_TURN = fitted(lambda u: np.cos(2 * np.pi * np.sqrt(u)), 1e-12, 0.25, 6)
-SIN_TURN = fitted(lambda u: np.sin(2 * np.pi * np.sqrt(u)) / np.sqrt(u), 1e-12, 0.25, 5)
-COS_HALF = fitted(lambda u: np.cos(0.075 * np.sqrt(u)), 0.99, 44.1, 3)
-SIN_HALF = fitted(lambda u: np.sin(0.075 * np.sqrt(u)) / np.sqrt(u), 0.99, 44.1, 3)
+COS_HALF = fitted(lambda u: 2 * np.cos(0.075 * np.sqrt(u)), 0.99, 44.1, 3)
+SIN_HALF = fitted(lambda u: 2 * np.sin(0.075 * np.sqrt(u)) / np.sqrt(u), 0.99, 44.1, 2)
+BASE = 1.0 / (4.0 * np.pi * 8.0)
+COS_BASE = fitted(lambda u: BASE * np.cos(2 * np.pi * np.sqrt(u)), 1e-12, 0.25, 5)
+SIN_BASE = fitted(lambda u: BASE * np.sin(2 * np.pi * np.sqrt(u)) / np.sqrt(u), 1e-12, 0.25, 5)
 
 
 def poly(coef, u):
@@ -54,7 +56,8 @@
 
 
 def body(
-    load_ref, blade_ref, src_ref, air_ref, reflect_ref, obs_ref, near_ref, out_ref,
+    load_in, blade_in, src_in, air_in, reflect_in, obs_in, near_in, out_ref,
+    load_ref, blade_ref, src_ref, air_ref, reflect_ref, obs_ref, near_ref, s_in,
     part, recv_x, own, recv_z, mine1, recv1, line2, mine2, recv2, spec,
     sx, rx, sz, rz, s1, r1, sl, rl, s2, r2, sf, rf,
 ):
@@ -81,13 +84,16 @@
         dy = (2 + q + q // 2 + 2 * (q // 3)) % 4
         return zl * 8 + ((y + dy) % 4) * 2 + (c + 1 - i % 2) % 2
 
-    half_peer = (x * 2 + (1 - zh), pi)
-
     def send(src, dst, ssem, rsem, to):
         return pltpu.make_async_remote_copy(
             src_ref=src, dst_ref=dst, send_sem=ssem, recv_sem=rsem, device_id=to, device_id_type=MESH
         )
 
+    outside = (load_in, src_in, air_in, obs_in, near_in, blade_in, reflect_in)
+    inside = (load_ref, src_ref, air_ref, obs_ref, near_ref, blade_ref, reflect_ref)
+    fetches = [pltpu.make_async_copy(a, b, s_in.at[n]) for n, (a, b) in enumerate(zip(outside, inside))]
+    for fetch in fetches:
+        fetch.start()
     barrier = pltpu.get_barrier_semaphore()
     peers = [x_peer(d) for d in (1, 2, 3)] + [z_peer(d) for d in range(1, 8)]
     peers += [(fi, block_panel(i)) for i in range(7)]
@@ -103,6 +109,8 @@
             return 0
 
         lax.fori_loop(0, 8, table_rows, 0)
+        for fetch in fetches:
+            fetch.wait()
         spectrum = jnp.dot(table[...], load_ref[...], preferred_element_type=F32) * (1.0 / 64.0)
         part[...] = spectrum.reshape(4, 64, LANES)
 
@@ -119,13 +127,12 @@
         wave = (8.0 + 0.15 * (F_DEV * fi.astype(F32) + 7.5)) * (1.0 / (2.0 * math.pi))
 
         def setup(state, targets, column, lift, start, stop):
-            def panel(k, _):
-                zz = k % 4
-                at = pl.multiple_of(block_panel(k // 4) * LANES, LANES)
-                tx, ty, tz = (targets[i : i + 1, pl.ds(at, LANES)] for i in range(3))
+            def block(i, _):
+                at = pl.multiple_of(block_panel(i) * LANES, LANES)
+                tx, ty, tz = (targets[n : n + 1, pl.ds(at, LANES)] for n in range(3))
                 tz = tz - lift
-                for h in range(LANES // ROWS):
-                    rows = pl.ds(h * ROWS, ROWS)
+                for h in range(512 // ROWS):
+                    zz, rows = h * ROWS // LANES, pl.ds(h * ROWS % LANES, ROWS)
                     dx, dy, dz = tx - column[zz, 0, rows, :], ty - column[zz, 1, rows, :], tz - column[zz, 2, rows, :]
                     square = dx * dx + dy * dy + dz * dz
                     inverse = lax.rsqrt(square)
@@ -133,25 +140,24 @@
                     turns = r * wave
                     turns = turns - jnp.round(turns)
                     u = turns * turns
-                    gain = inverse * (1.0 / (4.0 * math.pi))
-                    cp = poly(COS_TURN, u) * gain
-                    sp = poly(SIN_TURN, u) * (turns * gain)
+                    cp = poly(COS_BASE, u) * inverse
+                    sp = poly(SIN_BASE, u) * (turns * inverse)
                     c0 = poly(COS_HALF, square)
                     s0 = poly(SIN_HALF, square) * r
-                    twice = 4.0 * (c0 * c0) - 2.0
+                    twice = c0 * c0 - 2.0
                     c1, s1_ = (twice - 1.0) * c0, (twice + 1.0) * s0
                     c2, s2_ = twice * c1 - c0, twice * s1_ - s0
                     c3, s3 = twice * c2 - c1, twice * s2_ - s1_
                     cb, sb = c3 * c0 - s3 * s0, s3 * c0 + c3 * s0
                     cp, sp, cb, sb = (v.astype(BF16) for v in (cp, sp, cb, sb))
                     cc, ss, sc, cs = cp * cb, sp * sb, sp * cb, cp * sb
-                    dst = pl.ds(pl.multiple_of(k * LANES + h * ROWS, ROWS), ROWS)
+                    dst = pl.ds(pl.multiple_of(i * 512 + h * ROWS, ROWS), ROWS)
                     values = (cc + ss, sc - cs, cc - ss, sc + cs, c0, c1, c2, c3, s0, s1_, s2_, s3)
                     for n, v in enumerate(values):
                         state[n, dst, :] = v.astype(BF16)
                 return 0
 
-            lax.fori_loop(start, stop, panel, 0)
+            lax.fori_loop(start, stop, block, 0)
 
         setup1 = functools.partial(setup, state1, air_ref, column1, 3.0)
         setup2 = functools.partial(setup, state2, obs_ref, column2, 4.0)
@@ -167,7 +173,7 @@
         for s in x_sends:
             s.start()
 
-        setup1(CUT[0], 32)
+        setup1(CUT[0], 8)
         setup2(0, CUT[1])
 
         for s in x_sends:
@@ -264,30 +270,30 @@
         for s in l_sends:
             s.start()
 
-        setup2(CUT[2], 32)
-
-        def count(k, _):
-            at = pl.multiple_of(block_panel(k // 4) * LANES, LANES)
-            first = ((k % 4) * 8 + y * 2 + c) * LANES
-            index = lax.broadcasted_iota(jnp.int32, (LANES, LANES), 0)
-            total = jnp.zeros((LANES, LANES), F32)
-            for n in range(4):
-                total = total + jnp.where(index == near_ref[n : n + 1, pl.ds(at, LANES)] - first, 0.5, 0.0)
-            hits[pl.ds(pl.multiple_of(k * LANES, LANES), LANES), :] = total.astype(BF16)
+        setup2(CUT[2], 8)
+
+        def count(i, _):
+            at = pl.multiple_of(block_panel(i) * LANES, LANES)
+            near = [near_ref[n : n + 1, pl.ds(at, LANES)] - (y * 2 + c) * LANES for n in range(4)]
+            for zz in range(4):
+                index = lax.broadcasted_iota(jnp.int32, (LANES, LANES), 0) + zz * 8 * LANES
+                total = jnp.where(index == near[0], 0.5, 0.0)
+                for n in range(1, 4):
+                    total = total + jnp.where(index == near[n], 0.5, 0.0)
+                hits[pl.ds(pl.multiple_of(i * 512 + zz * LANES, LANES), LANES), :] = total.astype(BF16)
             return 0
 
-        lax.fori_loop(0, PANELS, count, 0)
+        lax.fori_loop(0, 8, count, 0)
 
         for s in l_sends:
             s.wait_recv()
         observed, sends2 = radiate(lambda zz: line2[zz], state2, mine2, recv2, s2, r2, True)
         spec[fi] = observed
 
-        f_sends = [send(spec.at[fi], spec.at[fi], sf.at[0], rf.at[0], half_peer)]
-        f_sends += [send(spec.at[fi], spec.at[fi], sf.at[d], rf.at[d], x_peer(d)) for d in (2, 1, 3)]
-        other = x * 2 + (1 - zh)
-        f_sends += [send(spec.at[other], spec.at[other], sf.at[3 + d], rf.at[3 + d], x_peer(d)) for d in (2, 1, 3)]
-        for s in f_sends[:4]:
+        f_sends = [
+            send(spec.at[fi], spec.at[fi], sf.at[d - 1], rf.at[d - 1], ((fi + d) % 8, pi)) for d in range(1, 8)
+        ]
+        for s in f_sends:
             s.start()
 
         def back_rows(i, _):
@@ -302,10 +308,7 @@
             return 0
 
         lax.fori_loop(0, T_DEV // 32, back_rows, 0)
-        f_sends[0].wait_recv()
-        for s in f_sends[4:]:
-            s.start()
-        for s in f_sends[1:]:
+        for s in f_sends:
             s.wait_recv()
 
         seen = spec[...].reshape(256, LANES) * (1.0 / 16.0)
@@ -333,22 +336,24 @@
 
 
 def on_device(load, blade, source, airframe, reflect, observer, near):
+    args = (load, blade.reshape(1, LANES), source, airframe, reflect.reshape(1, LANES), observer, near.T)
     vmem = pl.BlockSpec(memory_space=pltpu.VMEM)
     dma = pltpu.SemaphoreType.DMA
     slots = [(4, 64), (3, 64), (2, 32), (8, 32), (8, 32), (7, 32), (4, 32), (8, 32), (7, 32), (8, 32)]
-    scratch = [pltpu.VMEM((*slot, LANES), F32) for slot in slots]
+    scratch = [pltpu.VMEM(a.shape, a.dtype) for a in args] + [dma((7,))]
+    scratch += [pltpu.VMEM((*slot, LANES), F32) for slot in slots]
     scratch += [dma((n,)) for n in (3, 3, 7, 7, 7, 7, 3, 3, 7, 7, 7, 7)]
     return pl.pallas_call(
         body,
         out_shape=jax.ShapeDtypeStruct((T_DEV, LANES), F32),
-        in_specs=[vmem] * 7,
+        in_specs=[pl.BlockSpec(memory_space=pl.ANY)] * 7,
         out_specs=vmem,
         scratch_shapes=scratch,
         compiler_params=pltpu.CompilerParams(
             collective_id=0, has_side_effects=True, vmem_limit_bytes=56 * 1024 * 1024
         ),
         name="rotor",
-    )(load, blade.reshape(1, LANES), source, airframe, reflect.reshape(1, LANES), observer, near.T)
+    )(*args)
 
 
 def solution(mesh):

time: 53.6 us -> 47.8 us (0.89)
  Pallas kernels: 51.8 us -> 46 us
    pallas_call x1, Pallas kernels: 51.8 us -> 46 us  [on_device(): pl.pallas_call(body, out_shape=jax.ShapeDtypeStruct((T_DEV, LANES), F32),...]
where the time goes in v3:
time: 47.8 us; the launch traced here: 47.7 us
  Pallas kernels  46 us (96%)
  local copies, waits for them, and re-layouts  1.67 us (3%)
    pallas_call x1, Pallas kernels, on_device(): pl.pallas_call(body, out_shape=jax.ShapeDtypeStruct((T_DEV, LANES), F32),...  46 us
    unnamed x1, local copies, waits for them, and re-layouts  1.67 us

profile of v3, /device:TPU:8, one launch (start us, length us, event | category | flops | bytes accessed | tf_op | source)
XLA Modules:
  0.0 47.7 jit_solution(2382461303455725957)
XLA Ops:
  0.0 46.0 %rotor.1 = f32[512,128]{1,0:T(8,128)} custom-call(bf16[512,128]{1,0:T(8,128)(2,1)} %load_in.1, s32[1,128]{1,0:T(1,128)} %bitcast.4, f32[3,4096]{1,0:T(4,128)} %src_in.1, f32[3,4096]{1,0:T(4,128)} %air_in.1, f32[1,128]{1,0:T(1,128)} %bitcast.5, f32[3,4096]{1,0:T(4,128)} %obs_in.1, s32[4,4096]{1,0:T(4,128)} %bitcast.3), custom_call_target="tpu_custom_call" | custom-call | tf_op jit(solution)/shard_map/rotor/pallas_call | solution.py:346
  46.0 1.7 %copy.9 = f32[512,128]{1,0:T(8,128)} copy(f32[512,128]{1,0:T(8,128)} %rotor.1) | data formatting | bytes 524288

commit v4 on v3

--- a/solution.py
+++ b/solution.py
@@ -16,8 +16,8 @@
 LANES = 128
 T_DEV = 512
 F_DEV = 16
-CUT = (4, 1, 5)
-ROWS = 64
+CUT = (4, 2, 4)
+ROWS = 32
 
 
 def fitted(fn, low, high, degree):
@@ -56,8 +56,8 @@
 
 
 def body(
-    load_in, blade_in, src_in, air_in, reflect_in, obs_in, near_in, out_ref,
-    load_ref, blade_ref, src_ref, air_ref, reflect_ref, obs_ref, near_ref, s_in,
+    load_in, blade_in, src_in, air_in, reflect_in, obs_in, near_in, seen_ref, back_hi, back_lo,
+    load_ref, blade_ref, src_ref, air_ref, reflect_ref, obs_ref, near_ref, s_in, relay,
     part, recv_x, own, recv_z, mine1, recv1, line2, mine2, recv2, spec,
     sx, rx, sz, rz, s1, r1, sl, rl, s2, r2, sf, rf,
 ):
@@ -95,12 +95,12 @@
     for fetch in fetches:
         fetch.start()
     barrier = pltpu.get_barrier_semaphore()
-    peers = [x_peer(d) for d in (1, 2, 3)] + [z_peer(d) for d in range(1, 8)]
+    peers = [x_peer(d) for d in (1, 2, 3)] + [z_peer(d) for d in (1, 2, 6, 7)]
     peers += [(fi, block_panel(i)) for i in range(7)]
     for to in peers:
         pl.semaphore_signal(barrier, inc=1, device_id=to, device_id_type=MESH)
 
-    def work(table, state1, state2, hits, back_hi, back_lo, column1, column2, weights):
+    def work(table, state1, state2, hits, column1, column2, weights):
         def table_rows(i, _):
             row = lax.broadcasted_iota(jnp.int32, (32, T_DEV), 0)
             t = lax.broadcasted_iota(jnp.int32, (32, T_DEV), 1) + fi * T_DEV
@@ -161,10 +161,6 @@
 
         setup1 = functools.partial(setup, state1, air_ref, column1, 3.0)
         setup2 = functools.partial(setup, state2, obs_ref, column2, 4.0)
-        columns(column1, src_ref)
-        columns(column2, air_ref)
-
-        setup1(0, CUT[0])
         pl.semaphore_wait(barrier, len(peers))
 
         x_sends = [
@@ -172,9 +168,11 @@
         ]
         for s in x_sends:
             s.start()
-
-        setup1(CUT[0], 8)
-        setup2(0, CUT[1])
+        for d in (2, 6):
+            pl.semaphore_signal(relay, inc=1, device_id=z_peer(d), device_id_type=MESH)
+
+        columns(column1, src_ref)
+        setup1(0, CUT[0])
 
         for s in x_sends:
             s.wait_recv()
@@ -190,13 +188,16 @@
             send(own.at[z_of(d) // 4], recv_z.at[z], sz.at[d - 1], rz.at[d - 1], z_peer(d))
             for d in (4, 3, 5, 2, 6, 1, 7)
         ]
+        pl.semaphore_wait(relay, 2)
         for s in z_sends:
             s.start()
         recv_z[z] = own[zh]
 
-        setup2(CUT[1], CUT[2])
-
-        def radiate(line, state, mine, recv, ssem, rsem, near):
+        setup1(CUT[0], 8)
+        columns(column2, air_ref)
+        setup2(0, CUT[1])
+
+        def radiate(line, state, mine, recv, ssem, rsem, near, beside):
             row = lax.broadcasted_iota(jnp.int32, (32, LANES), 0)
             even = row % 2 == 0
             side = jnp.where((row // 2) % 2 == 0, 1.0, -1.0).astype(F32)
@@ -253,24 +254,13 @@
                 return 0
 
             lax.fori_loop(0, 8, block, 0)
+            beside()
             copies = [copy(i) for i in range(7)]
             total = mine[7]
             for i in range(7):
                 copies[i].wait_recv()
                 total = total + recv[i]
             return total, copies
-
-        for s in z_sends:
-            s.wait_recv()
-        incident, sends1 = radiate(lambda zz: recv_z[zz] + recv_z[zz + 4], state1, mine1, recv1, s1, r1, False)
-        line2[zl] = incident * reflect_ref[...]
-        l_sends = [
-            send(line2.at[zl], line2.at[zl], sl.at[d - 1], rl.at[d - 1], line_peer(d)) for d in (2, 1, 3)
-        ]
-        for s in l_sends:
-            s.start()
-
-        setup2(CUT[2], 8)
 
         def count(i, _):
             at = pl.multiple_of(block_panel(i) * LANES, LANES)
@@ -283,11 +273,26 @@
                 hits[pl.ds(pl.multiple_of(i * 512 + zz * LANES, LANES), LANES), :] = total.astype(BF16)
             return 0
 
-        lax.fori_loop(0, 8, count, 0)
+        def tail1():
+            lax.fori_loop(0, 8, count, 0)
+            setup2(CUT[1], CUT[2])
+
+        for s in z_sends:
+            s.wait_recv()
+        incident, sends1 = radiate(lambda zz: recv_z[zz] + recv_z[zz + 4], state1, mine1, recv1, s1, r1, False, tail1)
+        line2[zl] = incident * reflect_ref[...]
+        l_sends = [
+            send(line2.at[zl], line2.at[zl], sl.at[d - 1], rl.at[d - 1], line_peer(d)) for d in (2, 1, 3)
+        ]
+        for s in l_sends:
+            s.start()
+
+        setup2(CUT[2], 8)
+
 
         for s in l_sends:
             s.wait_recv()
-        observed, sends2 = radiate(lambda zz: line2[zz], state2, mine2, recv2, s2, r2, True)
+        observed, sends2 = radiate(lambda zz: line2[zz], state2, mine2, recv2, s2, r2, True, lambda: None)
         spec[fi] = observed
 
         f_sends = [
@@ -314,9 +319,7 @@
         seen = spec[...].reshape(256, LANES) * (1.0 / 16.0)
         hi = seen.astype(BF16)
         lo = (seen - hi.astype(F32)).astype(BF16)
-        wide = jnp.dot(back_hi[...], jnp.concatenate([hi, lo], axis=1), preferred_element_type=F32)
-        narrow = jnp.dot(back_lo[...], hi, preferred_element_type=F32)
-        out_ref[...] = wide[:, :LANES] + wide[:, LANES:] + narrow
+        seen_ref[...] = jnp.concatenate([hi, lo], axis=1)
 
         for s in x_sends + z_sends + sends1 + l_sends + sends2 + f_sends:
             s.wait_send()
@@ -327,33 +330,47 @@
         pltpu.VMEM((12, 4096, LANES), BF16),
         pltpu.VMEM((12, 4096, LANES), BF16),
         pltpu.VMEM((4096, LANES), BF16),
-        pltpu.VMEM((T_DEV, 256), BF16),
-        pltpu.VMEM((T_DEV, 256), BF16),
         pltpu.VMEM((4, 3, LANES, LANES), F32),
         pltpu.VMEM((4, 3, LANES, LANES), F32),
         pltpu.VMEM((2, 4, 16, 1024), BF16),
     )
 
 
+def back(seen_ref, hi_ref, lo_ref, out_ref):
+    wide = jnp.dot(hi_ref[...], seen_ref[...], preferred_element_type=F32)
+    narrow = jnp.dot(lo_ref[...], seen_ref[:, :LANES], preferred_element_type=F32)
+    out_ref[...] = wide[:, :LANES] + wide[:, LANES:] + narrow
+
+
 def on_device(load, blade, source, airframe, reflect, observer, near):
     args = (load, blade.reshape(1, LANES), source, airframe, reflect.reshape(1, LANES), observer, near.T)
+    args = tuple(pltpu.with_memory_space_constraint(a, pltpu.HBM) for a in args)
     vmem = pl.BlockSpec(memory_space=pltpu.VMEM)
     dma = pltpu.SemaphoreType.DMA
     slots = [(4, 64), (3, 64), (2, 32), (8, 32), (8, 32), (7, 32), (4, 32), (8, 32), (7, 32), (8, 32)]
-    scratch = [pltpu.VMEM(a.shape, a.dtype) for a in args] + [dma((7,))]
+    scratch = [pltpu.VMEM(a.shape, a.dtype) for a in args] + [dma((7,)), pltpu.SemaphoreType.REGULAR]
     scratch += [pltpu.VMEM((*slot, LANES), F32) for slot in slots]
     scratch += [dma((n,)) for n in (3, 3, 7, 7, 7, 7, 3, 3, 7, 7, 7, 7)]
-    return pl.pallas_call(
+    shapes = ((256, 256), (T_DEV, 256), (T_DEV, 256))
+    parts = pl.pallas_call(
         body,
-        out_shape=jax.ShapeDtypeStruct((T_DEV, LANES), F32),
-        in_specs=[pl.BlockSpec(memory_space=pl.ANY)] * 7,
-        out_specs=vmem,
+        out_shape=[jax.ShapeDtypeStruct(s, BF16) for s in shapes],
+        in_specs=[pl.BlockSpec(memory_space=pltpu.HBM)] * 7,
+        out_specs=[vmem] * 3,
         scratch_shapes=scratch,
         compiler_params=pltpu.CompilerParams(
-            collective_id=0, has_side_effects=True, vmem_limit_bytes=56 * 1024 * 1024
+            collective_id=0, has_side_effects=True, vmem_limit_bytes=40 * 1024 * 1024
         ),
         name="rotor",
     )(*args)
+    return pl.pallas_call(
+        back,
+        out_shape=jax.ShapeDtypeStruct((T_DEV, LANES), F32),
+        in_specs=[vmem] * 3,
+        out_specs=vmem,
+        compiler_params=pltpu.CompilerParams(vmem_limit_bytes=4 * 1024 * 1024),
+        name="back",
+    )(*parts)
 
 
 def solution(mesh):

time: 47.8 us -> 44.2 us (0.925)
  Pallas kernels: 46 us -> 44 us
  local copies, waits for them, and re-layouts: 1.67 us -> 0 us
    pallas_call x1 -> x2, Pallas kernels: 46 us -> 44 us  [the longest x1 43 us: on_device(): pl.pallas_call(body, out_shape=[jax.ShapeDtypeStruct(s, BF16) for s in sh...]
    unnamed x1 -> x0, local copies, waits for them, and re-layouts: 1.67 us -> none
where the time goes in v4:
time: 44.2 us; the launch traced here: 44 us
  Pallas kernels  44 us (100%)
    pallas_call x1, Pallas kernels, on_device(): pl.pallas_call(body, out_shape=[jax.ShapeDtypeStruct(s, BF16) for s in sh...  43 us
    pallas_call x1, Pallas kernels, on_device(): pl.pallas_call(back, out_shape=jax.ShapeDtypeStruct((T_DEV, LANES), F32),...  1.01 us

profile of v4, /device:TPU:8, one launch (start us, length us, event | category | flops | bytes accessed | tf_op | source)
XLA Modules:
  0.0 44.0 jit_solution(15398223202258580129)
XLA Ops:
  0.0 43.0 %rotor.1 = (bf16[256,256]{1,0:T(8,128)(2,1)S(1)}, bf16[512,256]{1,0:T(8,128)(2,1)S(1)}, bf16[512,256]{1,0:T(8,128)(2,1)S(1)}) custom-call(bf16[512,128]{1,0:T(8,128)(2,1)} %load_in.1, s32[1,128]{1,0:T(1,128)} %bitcast.4, f32[3,4096]{1,0:T(4,128)} %src_in.1, f32[3,4096]{1,0:T(4,128)} %air_in.1, f32[1,128]{1,0:T(1,128)} %bitcast.5, f32[3,4096]{1,0:T(4,128)} %obs_in.1, ...), custom_call_target="tpu_custom_call" | custom-call | tf_op jit(solution)/shard_map/rotor/pallas_call | solution.py:355
  43.0 1.0 %back.1 = f32[512,128]{1,0:T(8,128)} custom-call(bf16[256,256]{1,0:T(8,128)(2,1)S(1)} %get-tuple-element.8.seen_ref, bf16[512,256]{1,0:T(8,128)(2,1)S(1)} %get-tuple-element.9.hi_ref, bf16[512,256]{1,0:T(8,128)(2,1)S(1)} %get-tuple-element.10.lo_ref), custom_call_target="tpu_custom_call" | custom-call | tf_op jit(solution)/shard_map/back/pallas_call | solution.py:366

commit v5 on v4

--- a/solution.py
+++ b/solution.py
@@ -25,12 +25,12 @@
     return [float(v) for v in cheb.convert(kind=np.polynomial.Polynomial).coef]
 
 
-COS_TURN = fitted(lambda u: np.cos(2 * np.pi * np.sqrt(u)), 1e-12, 0.25, 6)
-COS_HALF = fitted(lambda u: 2 * np.cos(0.075 * np.sqrt(u)), 0.99, 44.1, 3)
+COS_TURN = fitted(lambda u: np.cos(2 * np.pi * np.sqrt(u)), 1e-12, 0.25, 5)
+COS_HALF = fitted(lambda u: 2 * np.cos(0.075 * np.sqrt(u)), 0.99, 44.1, 2)
 SIN_HALF = fitted(lambda u: 2 * np.sin(0.075 * np.sqrt(u)) / np.sqrt(u), 0.99, 44.1, 2)
 BASE = 1.0 / (4.0 * np.pi * 8.0)
 COS_BASE = fitted(lambda u: BASE * np.cos(2 * np.pi * np.sqrt(u)), 1e-12, 0.25, 5)
-SIN_BASE = fitted(lambda u: BASE * np.sin(2 * np.pi * np.sqrt(u)) / np.sqrt(u), 1e-12, 0.25, 5)
+SIN_BASE = fitted(lambda u: BASE * np.sin(2 * np.pi * np.sqrt(u)) / np.sqrt(u), 1e-12, 0.25, 4)
 
 
 def poly(coef, u):
@@ -265,12 +265,16 @@
         def count(i, _):
             at = pl.multiple_of(block_panel(i) * LANES, LANES)
             near = [near_ref[n : n + 1, pl.ds(at, LANES)] - (y * 2 + c) * LANES for n in range(4)]
+            index = lax.broadcasted_iota(jnp.int32, (LANES, LANES), 0).astype(F32).astype(BF16)
+            half, none = jnp.asarray(0.5, BF16), jnp.asarray(0.0, BF16)
             for zz in range(4):
-                index = lax.broadcasted_iota(jnp.int32, (LANES, LANES), 0) + zz * 8 * LANES
-                total = jnp.where(index == near[0], 0.5, 0.0)
-                for n in range(1, 4):
-                    total = total + jnp.where(index == near[n], 0.5, 0.0)
-                hits[pl.ds(pl.multiple_of(i * 512 + zz * LANES, LANES), LANES), :] = total.astype(BF16)
+                total = None
+                for n in range(4):
+                    local = near[n] - zz * 8 * LANES
+                    local = jnp.where((local >= 0) & (local < LANES), local, -1).astype(F32).astype(BF16)
+                    found = jnp.where(index == local, half, none)
+                    total = found if total is None else total + found
+                hits[pl.ds(pl.multiple_of(i * 512 + zz * LANES, LANES), LANES), :] = total
             return 0
 
         def tail1():
@@ -336,10 +340,17 @@
     )
 
 
-def back(seen_ref, hi_ref, lo_ref, out_ref):
-    wide = jnp.dot(hi_ref[...], seen_ref[...], preferred_element_type=F32)
-    narrow = jnp.dot(lo_ref[...], seen_ref[:, :LANES], preferred_element_type=F32)
-    out_ref[...] = wide[:, :LANES] + wide[:, LANES:] + narrow
+def back(seen_ref, hi_ref, lo_ref, out_ref, made, done):
+    copies = []
+    for q in range(4):
+        rows = pl.ds(q * LANES, LANES)
+        wide = jnp.dot(hi_ref[rows, :], seen_ref[...], preferred_element_type=F32)
+        narrow = jnp.dot(lo_ref[rows, :], seen_ref[:, :LANES], preferred_element_type=F32)
+        made[rows, :] = wide[:, :LANES] + wide[:, LANES:] + narrow
+        copies.append(pltpu.make_async_copy(made.at[rows], out_ref.at[rows], done.at[q]))
+        copies[q].start()
+    for copy in copies:
+        copy.wait()
 
 
 def on_device(load, blade, source, airframe, reflect, observer, near):
@@ -367,7 +378,8 @@
         back,
         out_shape=jax.ShapeDtypeStruct((T_DEV, LANES), F32),
         in_specs=[vmem] * 3,
-        out_specs=vmem,
+        out_specs=pl.BlockSpec(memory_space=pl.ANY),
+        scratch_shapes=[pltpu.VMEM((T_DEV, LANES), F32), dma((4,))],
         compiler_params=pltpu.CompilerParams(vmem_limit_bytes=4 * 1024 * 1024),
         name="back",
     )(*parts)

time: 44.2 us -> 43.7 us (0.989)
  Pallas kernels: 44 us -> 43.4 us
    pallas_call x1, Pallas kernels: 43 us -> 42.5 us  [on_device(): pl.pallas_call(body, out_shape=[jax.ShapeDtypeStruct(s, BF16) for s in sh...]
where the time goes in v5:
time: 43.7 us; the launch traced here: 43.4 us
  Pallas kernels  43.4 us (99%)
    pallas_call x1, Pallas kernels, on_device(): pl.pallas_call(body, out_shape=[jax.ShapeDtypeStruct(s, BF16) for s in sh...  42.5 us
    pallas_call x1, Pallas kernels, on_device(): pl.pallas_call(back, out_shape=jax.ShapeDtypeStruct((T_DEV, LANES), F32),...  0.96 us

profile of v5, /device:TPU:8, one launch (start us, length us, event | category | flops | bytes accessed | tf_op | source)
XLA Modules:
  0.0 43.4 jit_solution(17299863371239898080)
XLA Ops:
  0.0 42.5 %rotor.1 = (bf16[256,256]{1,0:T(8,128)(2,1)S(1)}, bf16[512,256]{1,0:T(8,128)(2,1)S(1)}, bf16[512,256]{1,0:T(8,128)(2,1)S(1)}) custom-call(bf16[512,128]{1,0:T(8,128)(2,1)} %load_in.1, s32[1,128]{1,0:T(1,128)} %bitcast.4, f32[3,4096]{1,0:T(4,128)} %src_in.1, f32[3,4096]{1,0:T(4,128)} %air_in.1, f32[1,128]{1,0:T(1,128)} %bitcast.5, f32[3,4096]{1,0:T(4,128)} %obs_in.1, ...), custom_call_target="tpu_custom_call" | custom-call | tf_op jit(solution)/shard_map/rotor/pallas_call | solution.py:366
  42.5 1.0 %back.1 = f32[512,128]{1,0:T(8,128)} custom-call(bf16[256,256]{1,0:T(8,128)(2,1)S(1)} %get-tuple-element.8.seen_ref, bf16[512,256]{1,0:T(8,128)(2,1)S(1)} %get-tuple-element.9.hi_ref, bf16[512,256]{1,0:T(8,128)(2,1)S(1)} %get-tuple-element.10.lo_ref), custom_call_target="tpu_custom_call" | custom-call | tf_op jit(solution)/shard_map/back/pallas_call | solution.py:377

commit v6 on v5

--- a/solution.py
+++ b/solution.py
@@ -16,7 +16,7 @@
 LANES = 128
 T_DEV = 512
 F_DEV = 16
-CUT = (4, 2, 4)
+CUT = (4, 2, 3)
 ROWS = 32
 
 

time: 43.7 us -> 43.2 us (0.989)
  no operation moved by 1% of the time
where the time goes in v6:
time: 43.2 us; the launch traced here: 43.1 us
  Pallas kernels  43 us (100%)
    pallas_call x1, Pallas kernels, on_device(): pl.pallas_call(body, out_shape=[jax.ShapeDtypeStruct(s, BF16) for s in sh...  42.1 us
    pallas_call x1, Pallas kernels, on_device(): pl.pallas_call(back, out_shape=jax.ShapeDtypeStruct((T_DEV, LANES), F32),...  0.96 us

profile of v6, /device:TPU:8, one launch (start us, length us, event | category | flops | bytes accessed | tf_op | source)
XLA Modules:
  0.0 43.1 jit_solution(18229070626993451056)
XLA Ops:
  0.0 42.1 %rotor.1 = (bf16[256,256]{1,0:T(8,128)(2,1)S(1)}, bf16[512,256]{1,0:T(8,128)(2,1)S(1)}, bf16[512,256]{1,0:T(8,128)(2,1)S(1)}) custom-call(bf16[512,128]{1,0:T(8,128)(2,1)} %load_in.1, s32[1,128]{1,0:T(1,128)} %bitcast.4, f32[3,4096]{1,0:T(4,128)} %src_in.1, f32[3,4096]{1,0:T(4,128)} %air_in.1, f32[1,128]{1,0:T(1,128)} %bitcast.5, f32[3,4096]{1,0:T(4,128)} %obs_in.1, ...), custom_call_target="tpu_custom_call" | custom-call | tf_op jit(solution)/shard_map/rotor/pallas_call | solution.py:366
  42.1 1.0 %back.1 = f32[512,128]{1,0:T(8,128)} custom-call(bf16[256,256]{1,0:T(8,128)(2,1)S(1)} %get-tuple-element.8.seen_ref, bf16[512,256]{1,0:T(8,128)(2,1)S(1)} %get-tuple-element.9.hi_ref, bf16[512,256]{1,0:T(8,128)(2,1)S(1)} %get-tuple-element.10.lo_ref), custom_call_target="tpu_custom_call" | custom-call | tf_op jit(solution)/shard_map/back/pallas_call | solution.py:377

commit v7 on v6

--- a/solution.py
+++ b/solution.py
@@ -92,13 +92,14 @@
     outside = (load_in, src_in, air_in, obs_in, near_in, blade_in, reflect_in)
     inside = (load_ref, src_ref, air_ref, obs_ref, near_ref, blade_ref, reflect_ref)
     fetches = [pltpu.make_async_copy(a, b, s_in.at[n]) for n, (a, b) in enumerate(zip(outside, inside))]
-    for fetch in fetches:
-        fetch.start()
+    fetches[0].start()
     barrier = pltpu.get_barrier_semaphore()
     peers = [x_peer(d) for d in (1, 2, 3)] + [z_peer(d) for d in (1, 2, 6, 7)]
     peers += [(fi, block_panel(i)) for i in range(7)]
     for to in peers:
         pl.semaphore_signal(barrier, inc=1, device_id=to, device_id_type=MESH)
+    for fetch in fetches[1:]:
+        fetch.start()
 
     def work(table, state1, state2, hits, column1, column2, weights):
         def table_rows(i, _):
@@ -109,8 +110,7 @@
             return 0
 
         lax.fori_loop(0, 8, table_rows, 0)
-        for fetch in fetches:
-            fetch.wait()
+        fetches[0].wait()
         spectrum = jnp.dot(table[...], load_ref[...], preferred_element_type=F32) * (1.0 / 64.0)
         part[...] = spectrum.reshape(4, 64, LANES)
 
@@ -171,6 +171,8 @@
         for d in (2, 6):
             pl.semaphore_signal(relay, inc=1, device_id=z_peer(d), device_id_type=MESH)
 
+        for fetch in fetches[1:]:
+            fetch.wait()
         columns(column1, src_ref)
         setup1(0, CUT[0])
 

time: 43.2 us -> 43.1 us (level)
  no operation moved by 1% of the time
where the time goes in v7:
time: 43.1 us; the launch traced here: 43 us
  Pallas kernels  43 us (100%)
    pallas_call x1, Pallas kernels, on_device(): pl.pallas_call(body, out_shape=[jax.ShapeDtypeStruct(s, BF16) for s in sh...  42.1 us
    pallas_call x1, Pallas kernels, on_device(): pl.pallas_call(back, out_shape=jax.ShapeDtypeStruct((T_DEV, LANES), F32),...  0.96 us

profile of v7, /device:TPU:8, one launch (start us, length us, event | category | flops | bytes accessed | tf_op | source)
XLA Modules:
  0.0 43.0 jit_solution(4512226711283934350)
XLA Ops:
  0.0 42.1 %rotor.1 = (bf16[256,256]{1,0:T(8,128)(2,1)S(1)}, bf16[512,256]{1,0:T(8,128)(2,1)S(1)}, bf16[512,256]{1,0:T(8,128)(2,1)S(1)}) custom-call(bf16[512,128]{1,0:T(8,128)(2,1)} %load_in.1, s32[1,128]{1,0:T(1,128)} %bitcast.4, f32[3,4096]{1,0:T(4,128)} %src_in.1, f32[3,4096]{1,0:T(4,128)} %air_in.1, f32[1,128]{1,0:T(1,128)} %bitcast.5, f32[3,4096]{1,0:T(4,128)} %obs_in.1, ...), custom_call_target="tpu_custom_call" | custom-call | tf_op jit(solution)/shard_map/rotor/pallas_call | solution.py:368
  42.1 1.0 %back.1 = f32[512,128]{1,0:T(8,128)} custom-call(bf16[256,256]{1,0:T(8,128)(2,1)S(1)} %get-tuple-element.8.seen_ref, bf16[512,256]{1,0:T(8,128)(2,1)S(1)} %get-tuple-element.9.hi_ref, bf16[512,256]{1,0:T(8,128)(2,1)S(1)} %get-tuple-element.10.lo_ref), custom_call_target="tpu_custom_call" | custom-call | tf_op jit(solution)/shard_map/back/pallas_call | solution.py:379
